TPU v7x, 32 devices: a whole 2x2x4 slice. The times are simulated.
32 devices in a mesh: ens: 2 (over y), lon: 4 (over z), lat: 2 (over x), ch: 2 (over core).
Axes of the slice: x: 2, y: 2, z: 4, core: 2. Of those that a mesh axis runs over, the one named last changes fastest.
Arguments:
- input_field: bfloat16 [256, 128, 128], P(('ens', 'lat', 'ch'), 'lon'), parts along dimension 0, may hold values from -6 to 6
- encoder_filter: bfloat16 [128, 4, 5], P(('lat', 'ch')), may hold values from -2.6875 to 2.6875
- row_owner: int32 [256], P(('ens', 'lat', 'ch')), parts along dimension 0, may hold values from 0 to 63, as said below
- encoder_weight: bfloat16 [512, 256], replicated, may hold values from -0.25 to 0.25
- disco_basis: bfloat16 [64, 4, 3, 17], P(('lat', 'ch')), may hold values from -1.5 to 1.5
- row_widths: int32 [64], P(('lat', 'ch')), may hold values from 1 to 8, as said below
- block_weights: bfloat16 [2, 1024, 256], replicated, may hold values from -0.1875 to 0.1875
- cotangent: bfloat16 [128, 64, 256], P(('ens', 'lat', 'ch'), 'lon'), parts along dimension 0, may hold values from -6 to 6
Outputs:
- state_out: bfloat16 [128, 64, 256], P(('ens', 'lat', 'ch'), 'lon'), parts along dimension 0
- latent_grad: bfloat16 [128, 64, 256], P(('ens', 'lat', 'ch'), 'lon'), parts along dimension 0
- block_grads: float32 [4, 1024, 256], P('ens', None, 'ch'), parts along dimension 0
- encoder_grad: float32 [1024, 256], P('ens', 'ch'), parts along dimension 0
There are 2 independent parts, one for each index of `ens`. A program takes and returns all parts, laid end to end along the dimension named above; an argument that names none is the same for every part. Nothing has to cross between parts.
Inputs may be any that keep to these rules, and one draw needn't show every extreme that they name: `row_owner`: input row p feeds latent row (p - 1) // 2, p // 2 or (p + 1) // 2, and every latent row is fed by 1 to 3 input rows. `row_widths`: the first and last rows have 8.
All inputs are finite; a program needn't handle non-finite values.
Results may differ from a plain program's by a relative error of at most 0.014.
Values may be sent and summed in bfloat16 or wider, within the bound.
A program may use at most 64 MiB of HBM per device.

v0:
```python
import math
import jax
import jax.numpy as jnp
from jax import lax
from jax.sharding import PartitionSpec as P

REACH = 8
TAP_REACH = 2


def passed_along(value, axis, steps):
    count = lax.axis_size(axis)
    pairs = [(source, (source + steps) % count) for source in range(count)]
    return lax.ppermute(value, axis, pairs)


def from_behind(block, axis, distance):
    devices = range(lax.axis_size(axis))
    route = [(i - distance, i) for i in devices if i - distance in devices]
    return lax.ppermute(block, axis, route)


def padded(block, sides, width, periodic):
    for axis, dim in sides:
        count = lax.axis_size(axis)
        forward = [(i, i + 1) for i in range(count - 1)]
        if periodic:
            forward.append((count - 1, 0))
        backward = [(target, source) for source, target in forward]
        low = lax.ppermute(
            lax.slice_in_dim(block, block.shape[dim] - width, None, axis=dim), axis, forward
        )
        high = lax.ppermute(lax.slice_in_dim(block, 0, width, axis=dim), axis, backward)
        block = jnp.concatenate([low, block, high], axis=dim)
    return block


def add_edges(middle, to_first, to_last):
    row_count = middle.shape[0]
    rest_pads = [(0, 0)] * (middle.ndim - 1)
    lower = jnp.pad(to_first, [(0, row_count - 1)] + rest_pads)
    upper = jnp.pad(to_last, [(row_count - 1, 0)] + rest_pads)
    return middle + lower + upper


def apply_basis(banded, extended, rows_dev):
    accumulated = None
    for shift_row in range(3):
        term = jnp.einsum(
            "ikjq,iqc->ijkc",
            banded[:, :, shift_row],
            extended[shift_row : shift_row + rows_dev],
            preferred_element_type=jnp.float32,
        )
        accumulated = term if accumulated is None else accumulated + term
    return accumulated


def spread_basis(banded, errors):
    pieces = [
        jnp.einsum(
            "ikjq,ijkc->iqc", banded[:, :, shift_row], errors, preferred_element_type=jnp.float32
        )
        for shift_row in range(3)
    ]
    first = jnp.pad(pieces[0], ((0, 2), (0, 0), (0, 0)))
    second = jnp.pad(pieces[1], ((1, 1), (0, 0), (0, 0)))
    third = jnp.pad(pieces[2], ((2, 0), (0, 0), (0, 0)))
    return first + second + third


def return_rims(spread, cols_dev):
    left_rim = spread[:, :REACH]
    right_rim = spread[:, REACH + cols_dev :]
    interior = spread[:, REACH : REACH + cols_dev]
    from_east = passed_along(left_rim.astype(jnp.bfloat16), "lon", -1).astype(left_rim.dtype)
    from_west = passed_along(right_rim.astype(jnp.bfloat16), "lon", 1).astype(right_rim.dtype)
    interior = interior + jnp.pad(from_west, ((0, 0), (0, cols_dev - REACH), (0, 0)))
    interior = interior + jnp.pad(from_east, ((0, 0), (cols_dev - REACH, 0), (0, 0)))
    row_total = interior.shape[0]
    from_above = from_behind(interior[0:1], ("lat", "ch"), -1)
    from_below = from_behind(interior[row_total - 1 :], ("lat", "ch"), 1)
    return add_edges(interior[1 : row_total - 1], from_below, from_above)


def per_device(
    input_field,
    encoder_filter,
    row_owner,
    encoder_weight,
    disco_basis,
    row_widths,
    block_weights,
    cotangent,
):
    rows_in, cols_in, in_width = input_field.shape
    rows_dev = rows_in // 2
    cols_dev = cols_in // 2
    basis_count = encoder_filter.shape[1]
    tap_count = encoder_filter.shape[2]
    channels = block_weights.shape[2]
    layers = block_weights.shape[0]
    cell_count = rows_dev * cols_dev
    extended_in = padded(input_field, (("lon", 1),), TAP_REACH, True)
    filter_values = encoder_filter.astype(jnp.float32)
    accumulated = jnp.zeros((rows_in, cols_dev, basis_count, in_width), jnp.float32)
    for tap_index in range(tap_count):
        sampled = extended_in[:, tap_index : tap_index + cols_in : 2, :]
        accumulated = (
            accumulated
            + sampled[:, :, None, :].astype(jnp.float32)
            * filter_values[:, None, :, tap_index, None]
        )
    filtered_in = accumulated.astype(jnp.bfloat16).reshape(
        rows_in, cols_dev * basis_count * in_width
    )
    first_row = lax.axis_index(("lat", "ch")) * rows_dev
    relative = row_owner - first_row + 1
    selector = (relative[None, :] == jnp.arange(rows_dev + 2, dtype=jnp.int32)[:, None]).astype(
        jnp.bfloat16
    )
    summed = jnp.dot(selector, filtered_in, preferred_element_type=jnp.float32)
    from_above = from_behind(summed[0:1].astype(jnp.bfloat16), ("lat", "ch"), -1).astype(
        jnp.float32
    )
    from_below = from_behind(summed[rows_dev + 1 :].astype(jnp.bfloat16), ("lat", "ch"), 1).astype(
        jnp.float32
    )
    regridded = add_edges(summed[1 : rows_dev + 1], from_below, from_above)
    latent_in = regridded.astype(jnp.bfloat16).reshape(cell_count, basis_count * in_width)
    current = jnp.dot(latent_in, encoder_weight, preferred_element_type=jnp.float32).astype(
        jnp.bfloat16
    )
    current = current.reshape(rows_dev, cols_dev, channels)
    offsets = jnp.abs(jnp.arange(2 * REACH + 1, dtype=jnp.int32) - REACH)
    keep = offsets[None, :] <= row_widths[:, None]
    masked = jnp.where(keep[:, None, None, :], disco_basis, jnp.zeros_like(disco_basis))
    ext_cols = cols_dev + 2 * REACH
    differences = (
        jnp.arange(ext_cols, dtype=jnp.int32)[None, :]
        - jnp.arange(cols_dev, dtype=jnp.int32)[:, None]
    )
    placement = (
        differences[:, :, None] == jnp.arange(2 * REACH + 1, dtype=jnp.int32)[None, None, :]
    ).astype(jnp.bfloat16)
    banded = jnp.einsum(
        "ikrt,jqt->ikrjq", masked, placement, preferred_element_type=jnp.float32
    ).astype(jnp.bfloat16)
    saved = []
    for layer_index in range(layers):
        rows_ext = padded(current, ((("lat", "ch"), 0),), 1, False)
        extended = padded(rows_ext, (("lon", 1),), REACH, True)
        features = (
            apply_basis(banded, extended, rows_dev)
            .astype(jnp.bfloat16)
            .reshape(cell_count, basis_count * channels)
        )
        preact = jnp.dot(features, block_weights[layer_index], preferred_element_type=jnp.float32)
        current = (
            current.astype(jnp.float32) + jax.nn.silu(preact).reshape(rows_dev, cols_dev, channels)
        ).astype(jnp.bfloat16)
        saved.append((features, preact))
    gradient = cotangent
    weight_terms = [None] * layers
    for layer_index in reversed(range(layers)):
        features, preact = saved[layer_index]
        sigma = jax.nn.sigmoid(preact)
        upstream = gradient.reshape(cell_count, channels).astype(jnp.float32)
        act_grad = (upstream * sigma * (1.0 + preact * (1.0 - sigma))).astype(jnp.bfloat16)
        weight_terms[layer_index] = lax.dot_general(
            features, act_grad, (((0,), (0,)), ((), ())), preferred_element_type=jnp.float32
        )
        errors = lax.dot_general(
            act_grad,
            block_weights[layer_index],
            (((1,), (1,)), ((), ())),
            preferred_element_type=jnp.float32,
        )
        errors = errors.astype(jnp.bfloat16).reshape(rows_dev, cols_dev, basis_count, channels)
        spread = spread_basis(banded, errors)
        returned = return_rims(spread, cols_dev)
        gradient = (gradient.astype(jnp.float32) + returned).astype(jnp.bfloat16)
    encoder_term = lax.dot_general(
        latent_in,
        gradient.reshape(cell_count, channels),
        (((0,), (0,)), ((), ())),
        preferred_element_type=jnp.float32,
    )
    block_stack = jnp.concatenate(weight_terms, axis=0)
    own_width = channels // lax.axis_size("ch")
    block_part, encoder_part = (
        lax.psum_scatter(
            block_stack.astype(jnp.bfloat16), "ch", scatter_dimension=1, tiled=True
        ).astype(jnp.float32),
        lax.psum_scatter(
            encoder_term.astype(jnp.bfloat16), "ch", scatter_dimension=1, tiled=True
        ).astype(jnp.float32),
    )
    block_sum, encoder_sum = lax.psum((block_part, encoder_part), ("lon", "lat"))
    cells_total = cell_count * lax.axis_size("lon") * lax.axis_size(("lat", "ch"))
    normalizer = 1.0 / math.sqrt(cells_total)
    block_grads = (block_sum * normalizer).reshape(layers, basis_count * channels, own_width)
    encoder_grad = encoder_sum * normalizer
    return (current, gradient, block_grads, encoder_grad)


def solution(mesh):
    placed = (
        P(("ens", "lat", "ch"), "lon", None),
        P(("lat", "ch"), None, None),
        P(("ens", "lat", "ch")),
        P(),
        P(("lat", "ch"), None, None, None),
        P(("lat", "ch")),
        P(),
        P(("ens", "lat", "ch"), "lon", None),
    )
    return jax.shard_map(
        per_device,
        mesh=mesh,
        in_specs=placed,
        out_specs=(
            P(("ens", "lat", "ch"), "lon", None),
            P(("ens", "lat", "ch"), "lon", None),
            P("ens", None, "ch"),
            P("ens", "ch"),
        ),
        check_vma=False,
    )
```

profile of v0, /device:TPU:0, one launch (start us, length us, event | category | flops | bytes accessed | tf_op | source)
XLA Modules:
  0.0 203.9 jit_solution(1901425106041720855)
XLA Ops:
  7.2 1.0 fusion.64
  8.2 3.1 %collective-permute-start = (bf16[32,2,128]{2,1,0:T(2,128)(2,1)S(1)}, bf16[32,2,128]{2,1,0:T(2,128)(2,1)S(1)}, u32[]{:S(2)}, u32[]{:S(2)}) collective-permute-start(bf16[32,2,128]{2,1,0:T(2,128)(2,1)S(1)} %get-tuple-element.25), channel_id=1, source_target_pairs={{0,4},{4,8},{8,12},{12,0},{1,5},{5,9},{9,13},{13,1},{2,6},{6,10},{... | collective-permute-start | bytes 49160 | tf_op jit(solution)/shard_map/ppermute | solution.py:30
  11.3 2.1 %collective-permute-start.1 = (bf16[32,2,128]{2,1,0:T(2,128)(2,1)S(1)}, bf16[32,2,128]{2,1,0:T(2,128)(2,1)S(1)}, u32[]{:S(2)}, u32[]{:S(2)}) collective-permute-start(bf16[32,2,128]{2,1,0:T(2,128)(2,1)S(1)} %get-tuple-element.26), channel_id=1, source_target_pairs={{4,0},{8,4},{12,8},{0,12},{5,1},{9,5},{13,9},{1,13},{6,2},{10,6},{... | collective-permute-start | bytes 49160 | tf_op jit(solution)/shard_map/ppermute | solution.py:33
  14.1 0.7 broadcast_compare_fusion
  14.8 0.8 select_bitcast_fusion
  16.3 1.8 slice.167
  20.8 1.0 add_convert_fusion
  22.5 1.5 collective-permute-start.2
  24.0 1.3 collective-permute-start.3
  25.3 3.5 %collective-permute-done.3 = bf16[1,8192]{1,0:T(2,128)(2,1)S(1)} collective-permute-done((bf16[1,8192]{1,0:T(2,128)(2,1)S(1)}, bf16[1,8192]{1,0:T(2,128)(2,1)S(1)}, u32[]{:S(2)}, u32[]{:S(2)}) %collective-permute-start.3) | collective-permute-done | bytes 16416 | tf_op jit(solution)/shard_map/ppermute | solution.py:20
  29.3 4.5 %collective-permute-start.4 = (bf16[1,16,256]{2,1,0:T(8,128)(2,1)S(1)}, bf16[1,16,256]{2,1,0:T(8,128)(2,1)S(1)}, u32[]{:S(2)}, u32[]{:S(2)}) collective-permute-start(bf16[1,16,256]{2,1,0:T(8,128)(2,1)S(1)} %get-tuple-element.33), channel_id=1, source_target_pairs={{0,1},{1,2},{2,3},{4,5},{5,6},{6,7},{8,9},{9,10},{10,11},{12,13},{... | collective-permute-start | bytes 24584 | tf_op jit(solution)/shard_map/ppermute | solution.py:30
  33.9 1.3 collective-permute-start.5
  35.6 1.4 collective-permute-done.5
  37.1 3.8 %collective-permute-start.7 = (bf16[18,8,256]{2,1,0:T(8,128)(2,1)S(1)}, bf16[18,8,256]{2,1,0:T(8,128)(2,1)S(1)}, u32[]{:S(2)}, u32[]{:S(2)}) collective-permute-start(bf16[18,8,256]{2,1,0:T(8,128)(2,1)S(1)} %get-tuple-element.30), channel_id=1, source_target_pairs={{4,0},{8,4},{12,8},{0,12},{5,1},{9,5},{13,9},{1,13},{6,2},{10,6},{... | collective-permute-start | bytes 221192 | tf_op jit(solution)/shard_map/ppermute | solution.py:33
  41.0 2.3 %collective-permute-done.6 = bf16[18,8,256]{2,1,0:T(8,128)(2,1)S(1)} collective-permute-done((bf16[18,8,256]{2,1,0:T(8,128)(2,1)S(1)}, bf16[18,8,256]{2,1,0:T(8,128)(2,1)S(1)}, u32[]{:S(2)}, u32[]{:S(2)}) %collective-permute-start.6) | collective-permute-done | bytes 73760 | tf_op jit(solution)/shard_map/ppermute | solution.py:30
  44.6 0.8 copy-done.1
  45.4 1.0 fusion.37
  46.5 3.2 %collective-permute-start.8 = (bf16[1,16,256]{2,1,0:T(8,128)(2,1)S(1)}, bf16[1,16,256]{2,1,0:T(8,128)(2,1)S(1)}, u32[]{:S(2)}, u32[]{:S(2)}) collective-permute-start(bf16[1,16,256]{2,1,0:T(8,128)(2,1)S(1)} %get-tuple-element.31), channel_id=1, source_target_pairs={{0,1},{1,2},{2,3},{4,5},{5,6},{6,7},{8,9},{9,10},{10,11},{12,13},{... | collective-permute-start | bytes 24584 | tf_op jit(solution)/shard_map/ppermute | solution.py:30
  49.7 1.3 collective-permute-start.9
  51.0 1.8 collective-permute-done.9
  52.9 3.9 %collective-permute-start.11 = (bf16[18,8,256]{2,1,0:T(8,128)(2,1)S(1)}, bf16[18,8,256]{2,1,0:T(8,128)(2,1)S(1)}, u32[]{:S(2)}, u32[]{:S(2)}) collective-permute-start(bf16[18,8,256]{2,1,0:T(8,128)(2,1)S(1)} %get-tuple-element.28), channel_id=1, source_target_pairs={{4,0},{8,4},{12,8},{0,12},{5,1},{9,5},{13,9},{1,13},{6,2},{10,6},{... | collective-permute-start | bytes 221192 | tf_op jit(solution)/shard_map/ppermute | solution.py:33
  56.8 2.4 %collective-permute-done.10 = bf16[18,8,256]{2,1,0:T(8,128)(2,1)S(1)} collective-permute-done((bf16[18,8,256]{2,1,0:T(8,128)(2,1)S(1)}, bf16[18,8,256]{2,1,0:T(8,128)(2,1)S(1)}, u32[]{:S(2)}, u32[]{:S(2)}) %collective-permute-start.10) | collective-permute-done | bytes 73760 | tf_op jit(solution)/shard_map/ppermute | solution.py:30
  61.0 1.1 fusion.35
  64.5 1.3 collective-permute-start.12
  65.8 2.7 %collective-permute-start.13 = (bf16[18,8,256]{2,1,0:T(8,128)(2,1)S(1)}, bf16[18,8,256]{2,1,0:T(8,128)(2,1)S(1)}, u32[]{:S(2)}, u32[]{:S(2)}) collective-permute-start(bf16[18,8,256]{2,1,0:T(8,128)(2,1)S(1)} %get-tuple-element.22), channel_id=1, source_target_pairs={{0,12},{4,0},{8,4},{12,8},{1,13},{5,1},{9,5},{13,9},{2,14},{6,2},{... | collective-permute-start | bytes 221192 | tf_op jit(solution)/shard_map/ppermute | solution.py:14
  68.5 2.4 %collective-permute-done.12 = bf16[18,8,256]{2,1,0:T(8,128)(2,1)S(1)} collective-permute-done((bf16[18,8,256]{2,1,0:T(8,128)(2,1)S(1)}, bf16[18,8,256]{2,1,0:T(8,128)(2,1)S(1)}, u32[]{:S(2)}, u32[]{:S(2)}) %collective-permute-start.12) | collective-permute-done | bytes 73760 | tf_op jit(solution)/shard_map/ppermute | solution.py:14
  70.9 1.9 collective-permute-done.13
  72.9 2.1 %collective-permute-start.14 = (f32[1,16,256]{2,1,0:T(8,128)S(1)}, f32[1,16,256]{2,1,0:T(8,128)S(1)}, u32[]{:S(2)}, u32[]{:S(2)}) collective-permute-start(f32[1,16,256]{2,1,0:T(8,128)S(1)} %get-tuple-element.19), channel_id=1, source_target_pairs={{0,1},{1,2},{2,3},{4,5},{5,6},{6,7},{8,9},{9,10},{10,11},{12,13},{... | collective-permute-start | bytes 49160 | tf_op jit(solution)/shard_map/ppermute | solution.py:20
  74.9 1.3 collective-permute-start.15
  76.2 1.8 collective-permute-done.15
  78.2 1.1 convolution_convert_fusion.3
  79.4 1.4 reshape.128
  81.8 1.1 collective-permute-start.16
  83.0 2.8 %collective-permute-start.17 = (bf16[18,8,256]{2,1,0:T(8,128)(2,1)S(1)}, bf16[18,8,256]{2,1,0:T(8,128)(2,1)S(1)}, u32[]{:S(2)}, u32[]{:S(2)}) collective-permute-start(bf16[18,8,256]{2,1,0:T(8,128)(2,1)S(1)} %get-tuple-element.18), channel_id=1, source_target_pairs={{0,12},{4,0},{8,4},{12,8},{1,13},{5,1},{9,5},{13,9},{2,14},{6,2},{... | collective-permute-start | bytes 221192 | tf_op jit(solution)/shard_map/ppermute | solution.py:14
  85.7 2.4 %collective-permute-done.16 = bf16[18,8,256]{2,1,0:T(8,128)(2,1)S(1)} collective-permute-done((bf16[18,8,256]{2,1,0:T(8,128)(2,1)S(1)}, bf16[18,8,256]{2,1,0:T(8,128)(2,1)S(1)}, u32[]{:S(2)}, u32[]{:S(2)}) %collective-permute-start.16) | collective-permute-done | bytes 73760 | tf_op jit(solution)/shard_map/ppermute | solution.py:14
  88.2 3.7 %collective-permute-start.18 = (f32[1,16,256]{2,1,0:T(8,128)S(1)}, f32[1,16,256]{2,1,0:T(8,128)S(1)}, u32[]{:S(2)}, u32[]{:S(2)}) collective-permute-start(f32[1,16,256]{2,1,0:T(8,128)S(1)} %get-tuple-element.15), channel_id=1, source_target_pairs={{0,1},{1,2},{2,3},{4,5},{5,6},{6,7},{8,9},{9,10},{10,11},{12,13},{... | collective-permute-start | bytes 49160 | tf_op jit(solution)/shard_map/ppermute | solution.py:20
  92.0 1.4 collective-permute-start.19
  93.4 1.9 collective-permute-done.19
  95.6 0.8 copy.106
  97.4 1.4 copy.104
  98.8 0.9 copy-done.7
  100.4 6.6 %reduce-scatter.9.cloned.1.call-done = bf16[128,512]{1,0:T(8,128)(2,1)} async-done(((bf16[256,512]{1,0:T(8,128)(2,1)}), bf16[128,512]{1,0:T(8,128)(2,1)}) %reduce-scatter.9.cloned.1.call-update) | async-done | bytes 131088
  107.0 1.0 copy.107
  108.0 11.3 %reduce-scatter.7.cloned.1.call-done = bf16[128,2048]{1,0:T(8,128)(2,1)} async-done(((bf16[256,2048]{1,0:T(8,128)(2,1)}), bf16[128,2048]{1,0:T(8,128)(2,1)}) %reduce-scatter.7.cloned.1.call-update) | async-done | bytes 524304
  119.3 1.3 copy.105
  120.6 74.7 %all-reduce.18 = (f32[2048,128]{1,0:T(8,128)S(1)}, f32[512,128]{1,0:T(8,128)S(1)}) all-reduce(bf16[2048,128]{1,0:T(8,128)(2,1)S(1)} %copy.105, bf16[512,128]{1,0:T(8,128)(2,1)S(1)} %copy.107), channel_id=1, replica_groups=mesh['ens'=2,'lon'=4,'lat'=2,'ch'=2] {'lon','lat'}, use_global_device_ids=true, to_apply=%region_1.2 | all-reduce | flops 327680 | bytes 1966080 | tf_op jit(solution)/shard_map/psum | solution.py:199
  195.3 1.0 broadcast_multiply_fusion
  196.4 0.7 broadcast_multiply_fusion.1
  (107 shorter events, 14.3 us)
Async XLA Ops:
  7.2 21.9 %copy-start = (bf16[512,256]{1,0:T(8,128)(2,1)S(1)}, bf16[512,256]{1,0:T(8,128)(2,1)}, u32[]{:S(2)}) copy-start(bf16[512,256]{1,0:T(8,128)(2,1)} %param.11) | copy-start | bytes 786436
  7.2 11.5 %copy-start.3 = (bf16[32,32,128]{2,1,0:T(8,128)(2,1)S(1)}, bf16[32,32,128]{2,1,0:T(8,128)(2,1)}, u32[]{:S(2)}) copy-start(bf16[32,32,128]{2,1,0:T(8,128)(2,1)} %param.8) | copy-start | bytes 786436
  7.2 99.8 %reduce-scatter.9.cloned.1.call-start = ((), (), s32[]{:S(2)}) async-start(), calls=%async_computation.3 | async-start | bytes 393216
  8.2 10.4 %collective-permute-start = (bf16[32,2,128]{2,1,0:T(2,128)(2,1)S(1)}, bf16[32,2,128]{2,1,0:T(2,128)(2,1)S(1)}, u32[]{:S(2)}, u32[]{:S(2)}) collective-permute-start(bf16[32,2,128]{2,1,0:T(2,128)(2,1)S(1)} %get-tuple-element.25), channel_id=1, source_target_pairs={{0,4},{4,8},{8,12},{12,0},{1,5},{5,9},{9,13},{13,1},{2,6},{6,10},{... | collective-permute-start | bytes 49160 | tf_op jit(solution)/shard_map/ppermute | solution.py:30
  11.3 7.3 %collective-permute-start.1 = (bf16[32,2,128]{2,1,0:T(2,128)(2,1)S(1)}, bf16[32,2,128]{2,1,0:T(2,128)(2,1)S(1)}, u32[]{:S(2)}, u32[]{:S(2)}) collective-permute-start(bf16[32,2,128]{2,1,0:T(2,128)(2,1)S(1)} %get-tuple-element.26), channel_id=1, source_target_pairs={{4,0},{8,4},{12,8},{0,12},{5,1},{9,5},{13,9},{1,13},{6,2},{10,6},{... | collective-permute-start | bytes 49160 | tf_op jit(solution)/shard_map/ppermute | solution.py:33
  22.5 2.8 %collective-permute-start.2 = (bf16[1,8192]{1,0:T(2,128)(2,1)S(1)}, bf16[1,8192]{1,0:T(2,128)(2,1)S(1)}, u32[]{:S(2)}, u32[]{:S(2)}) collective-permute-start(bf16[1,8192]{1,0:T(2,128)(2,1)S(1)} %get-tuple-element.13), channel_id=1, source_target_pairs={{0,1},{1,2},{2,3},{4,5},{5,6},{6,7},{8,9},{9,10},{10,11},{12,13},{... | collective-permute-start | bytes 49160 | tf_op jit(solution)/shard_map/ppermute | solution.py:20
  24.0 4.8 %collective-permute-start.3 = (bf16[1,8192]{1,0:T(2,128)(2,1)S(1)}, bf16[1,8192]{1,0:T(2,128)(2,1)S(1)}, u32[]{:S(2)}, u32[]{:S(2)}) collective-permute-start(bf16[1,8192]{1,0:T(2,128)(2,1)S(1)} %get-tuple-element.14), channel_id=1, source_target_pairs={{1,0},{2,1},{3,2},{5,4},{6,5},{7,6},{9,8},{10,9},{11,10},{13,12},{... | collective-permute-start | bytes 49160 | tf_op jit(solution)/shard_map/ppermute | solution.py:20
  29.3 6.2 %collective-permute-start.4 = (bf16[1,16,256]{2,1,0:T(8,128)(2,1)S(1)}, bf16[1,16,256]{2,1,0:T(8,128)(2,1)S(1)}, u32[]{:S(2)}, u32[]{:S(2)}) collective-permute-start(bf16[1,16,256]{2,1,0:T(8,128)(2,1)S(1)} %get-tuple-element.33), channel_id=1, source_target_pairs={{0,1},{1,2},{2,3},{4,5},{5,6},{6,7},{8,9},{9,10},{10,11},{12,13},{... | collective-permute-start | bytes 24584 | tf_op jit(solution)/shard_map/ppermute | solution.py:30
  33.9 3.1 %collective-permute-start.5 = (bf16[1,16,256]{2,1,0:T(8,128)(2,1)S(1)}, bf16[1,16,256]{2,1,0:T(8,128)(2,1)S(1)}, u32[]{:S(2)}, u32[]{:S(2)}) collective-permute-start(bf16[1,16,256]{2,1,0:T(8,128)(2,1)S(1)} %get-tuple-element.34), channel_id=1, source_target_pairs={{1,0},{2,1},{3,2},{5,4},{6,5},{7,6},{9,8},{10,9},{11,10},{13,12},{... | collective-permute-start | bytes 24584 | tf_op jit(solution)/shard_map/ppermute | solution.py:33
  37.0 6.3 %collective-permute-start.6 = (bf16[18,8,256]{2,1,0:T(8,128)(2,1)S(1)}, bf16[18,8,256]{2,1,0:T(8,128)(2,1)S(1)}, u32[]{:S(2)}, u32[]{:S(2)}) collective-permute-start(bf16[18,8,256]{2,1,0:T(8,128)(2,1)S(1)} %get-tuple-element.29), channel_id=1, source_target_pairs={{0,4},{4,8},{8,12},{12,0},{1,5},{5,9},{9,13},{13,1},{2,6},{6,10},{... | collective-permute-start | bytes 221192 | tf_op jit(solution)/shard_map/ppermute | solution.py:30
  37.1 6.2 %collective-permute-start.7 = (bf16[18,8,256]{2,1,0:T(8,128)(2,1)S(1)}, bf16[18,8,256]{2,1,0:T(8,128)(2,1)S(1)}, u32[]{:S(2)}, u32[]{:S(2)}) collective-permute-start(bf16[18,8,256]{2,1,0:T(8,128)(2,1)S(1)} %get-tuple-element.30), channel_id=1, source_target_pairs={{4,0},{8,4},{12,8},{0,12},{5,1},{9,5},{13,9},{1,13},{6,2},{10,6},{... | collective-permute-start | bytes 221192 | tf_op jit(solution)/shard_map/ppermute | solution.py:33
  44.2 1.2 copy-start.1
  46.5 4.5 %collective-permute-start.8 = (bf16[1,16,256]{2,1,0:T(8,128)(2,1)S(1)}, bf16[1,16,256]{2,1,0:T(8,128)(2,1)S(1)}, u32[]{:S(2)}, u32[]{:S(2)}) collective-permute-start(bf16[1,16,256]{2,1,0:T(8,128)(2,1)S(1)} %get-tuple-element.31), channel_id=1, source_target_pairs={{0,1},{1,2},{2,3},{4,5},{5,6},{6,7},{8,9},{9,10},{10,11},{12,13},{... | collective-permute-start | bytes 24584 | tf_op jit(solution)/shard_map/ppermute | solution.py:30
  49.7 3.1 %collective-permute-start.9 = (bf16[1,16,256]{2,1,0:T(8,128)(2,1)S(1)}, bf16[1,16,256]{2,1,0:T(8,128)(2,1)S(1)}, u32[]{:S(2)}, u32[]{:S(2)}) collective-permute-start(bf16[1,16,256]{2,1,0:T(8,128)(2,1)S(1)} %get-tuple-element.32), channel_id=1, source_target_pairs={{1,0},{2,1},{3,2},{5,4},{6,5},{7,6},{9,8},{10,9},{11,10},{13,12},{... | collective-permute-start | bytes 24584 | tf_op jit(solution)/shard_map/ppermute | solution.py:33
  52.9 6.3 %collective-permute-start.10 = (bf16[18,8,256]{2,1,0:T(8,128)(2,1)S(1)}, bf16[18,8,256]{2,1,0:T(8,128)(2,1)S(1)}, u32[]{:S(2)}, u32[]{:S(2)}) collective-permute-start(bf16[18,8,256]{2,1,0:T(8,128)(2,1)S(1)} %get-tuple-element.27), channel_id=1, source_target_pairs={{0,4},{4,8},{8,12},{12,0},{1,5},{5,9},{9,13},{13,1},{2,6},{6,10},{... | collective-permute-start | bytes 221192 | tf_op jit(solution)/shard_map/ppermute | solution.py:30
  52.9 6.2 %collective-permute-start.11 = (bf16[18,8,256]{2,1,0:T(8,128)(2,1)S(1)}, bf16[18,8,256]{2,1,0:T(8,128)(2,1)S(1)}, u32[]{:S(2)}, u32[]{:S(2)}) collective-permute-start(bf16[18,8,256]{2,1,0:T(8,128)(2,1)S(1)} %get-tuple-element.28), channel_id=1, source_target_pairs={{4,0},{8,4},{12,8},{0,12},{5,1},{9,5},{13,9},{1,13},{6,2},{10,6},{... | collective-permute-start | bytes 221192 | tf_op jit(solution)/shard_map/ppermute | solution.py:33
  60.1 0.9 copy-start.9
  62.1 0.7 copy-start.4
  64.5 13.6 %copy-start.10 = (bf16[16,16,256]{2,1,0:T(8,128)(2,1)S(1)}, bf16[16,16,256]{2,1,0:T(8,128)(2,1)}, u32[]{:S(2)}) copy-start(bf16[16,16,256]{2,1,0:T(8,128)(2,1)} %param.15) | copy-start | bytes 393220
  64.5 13.6 %copy-start.8 = (f32[256,256]{1,0:T(8,128)S(1)}, f32[256,256]{1,0:T(8,128)}, u32[]{:S(2)}) copy-start(f32[256,256]{1,0:T(8,128)} %get-tuple-element.43) | copy-start | bytes 786436
  64.5 6.4 %collective-permute-start.12 = (bf16[18,8,256]{2,1,0:T(8,128)(2,1)S(1)}, bf16[18,8,256]{2,1,0:T(8,128)(2,1)S(1)}, u32[]{:S(2)}, u32[]{:S(2)}) collective-permute-start(bf16[18,8,256]{2,1,0:T(8,128)(2,1)S(1)} %get-tuple-element.21), channel_id=1, source_target_pairs={{0,4},{4,8},{8,12},{12,0},{1,5},{5,9},{9,13},{13,1},{2,6},{6,10},{... | collective-permute-start | bytes 221192 | tf_op jit(solution)/shard_map/ppermute | solution.py:14
  65.8 7.0 %collective-permute-start.13 = (bf16[18,8,256]{2,1,0:T(8,128)(2,1)S(1)}, bf16[18,8,256]{2,1,0:T(8,128)(2,1)S(1)}, u32[]{:S(2)}, u32[]{:S(2)}) collective-permute-start(bf16[18,8,256]{2,1,0:T(8,128)(2,1)S(1)} %get-tuple-element.22), channel_id=1, source_target_pairs={{0,12},{4,0},{8,4},{12,8},{1,13},{5,1},{9,5},{13,9},{2,14},{6,2},{... | collective-permute-start | bytes 221192 | tf_op jit(solution)/shard_map/ppermute | solution.py:14
  72.8 5.4 %copy-start.2 = (bf16[2,1024,256]{2,1,0:T(8,128)(2,1)S(1)}, bf16[2,1024,256]{2,1,0:T(8,128)(2,1)}, u32[]{:S(2)}) copy-start(bf16[2,1024,256]{2,1,0:T(8,128)(2,1)} %param.14) | copy-start | bytes 3145732
  72.9 3.4 %collective-permute-start.14 = (f32[1,16,256]{2,1,0:T(8,128)S(1)}, f32[1,16,256]{2,1,0:T(8,128)S(1)}, u32[]{:S(2)}, u32[]{:S(2)}) collective-permute-start(f32[1,16,256]{2,1,0:T(8,128)S(1)} %get-tuple-element.19), channel_id=1, source_target_pairs={{0,1},{1,2},{2,3},{4,5},{5,6},{6,7},{8,9},{9,10},{10,11},{12,13},{... | collective-permute-start | bytes 49160 | tf_op jit(solution)/shard_map/ppermute | solution.py:20
  74.9 3.1 %collective-permute-start.15 = (f32[1,16,256]{2,1,0:T(8,128)S(1)}, f32[1,16,256]{2,1,0:T(8,128)S(1)}, u32[]{:S(2)}, u32[]{:S(2)}) collective-permute-start(f32[1,16,256]{2,1,0:T(8,128)S(1)} %get-tuple-element.20), channel_id=1, source_target_pairs={{1,0},{2,1},{3,2},{5,4},{6,5},{7,6},{9,8},{10,9},{11,10},{13,12},{... | collective-permute-start | bytes 49160 | tf_op jit(solution)/shard_map/ppermute | solution.py:20
  81.8 6.3 %collective-permute-start.16 = (bf16[18,8,256]{2,1,0:T(8,128)(2,1)S(1)}, bf16[18,8,256]{2,1,0:T(8,128)(2,1)S(1)}, u32[]{:S(2)}, u32[]{:S(2)}) collective-permute-start(bf16[18,8,256]{2,1,0:T(8,128)(2,1)S(1)} %get-tuple-element.17), channel_id=1, source_target_pairs={{0,4},{4,8},{8,12},{12,0},{1,5},{5,9},{9,13},{13,1},{2,6},{6,10},{... | collective-permute-start | bytes 221192 | tf_op jit(solution)/shard_map/ppermute | solution.py:14
  83.0 5.2 %collective-permute-start.17 = (bf16[18,8,256]{2,1,0:T(8,128)(2,1)S(1)}, bf16[18,8,256]{2,1,0:T(8,128)(2,1)S(1)}, u32[]{:S(2)}, u32[]{:S(2)}) collective-permute-start(bf16[18,8,256]{2,1,0:T(8,128)(2,1)S(1)} %get-tuple-element.18), channel_id=1, source_target_pairs={{0,12},{4,0},{8,4},{12,8},{1,13},{5,1},{9,5},{13,9},{2,14},{6,2},{... | collective-permute-start | bytes 221192 | tf_op jit(solution)/shard_map/ppermute | solution.py:14
  88.2 5.2 %collective-permute-start.18 = (f32[1,16,256]{2,1,0:T(8,128)S(1)}, f32[1,16,256]{2,1,0:T(8,128)S(1)}, u32[]{:S(2)}, u32[]{:S(2)}) collective-permute-start(f32[1,16,256]{2,1,0:T(8,128)S(1)} %get-tuple-element.15), channel_id=1, source_target_pairs={{0,1},{1,2},{2,3},{4,5},{5,6},{6,7},{8,9},{9,10},{10,11},{12,13},{... | collective-permute-start | bytes 49160 | tf_op jit(solution)/shard_map/ppermute | solution.py:20
  91.9 4.6 %copy-start.5 = (bf16[256,256]{1,0:T(8,128)(2,1)S(1)}, bf16[256,256]{1,0:T(8,128)(2,1)}, u32[]{:S(2)}) copy-start(bf16[256,256]{1,0:T(8,128)(2,1)} %copy-done.4) | copy-start | bytes 393220
  92.0 3.3 %collective-permute-start.19 = (f32[1,16,256]{2,1,0:T(8,128)S(1)}, f32[1,16,256]{2,1,0:T(8,128)S(1)}, u32[]{:S(2)}, u32[]{:S(2)}) collective-permute-start(f32[1,16,256]{2,1,0:T(8,128)S(1)} %get-tuple-element.16), channel_id=1, source_target_pairs={{1,0},{2,1},{3,2},{5,4},{6,5},{7,6},{9,8},{10,9},{11,10},{13,12},{... | collective-permute-start | bytes 49160 | tf_op jit(solution)/shard_map/ppermute | solution.py:20
  95.3 1.6 copy-start.6
  96.5 22.8 %reduce-scatter.7.cloned.1.call-start = ((), (), s32[]{:S(2)}) async-start(), calls=%async_computation.2 | async-start | bytes 1572864
  98.8 0.9 copy-start.7
Sparse Core Ops, SparseCore 0:
  96.6 10.3 reduce-scatter.8
  109.8 9.4 reduce-scatter.6
where the time goes:
time: 205 us; the launch traced here: 204 us
  blocking collectives  74.7 us (36%)
  starting transfers between devices  42.6 us (21%)
  waiting for transfers between devices  39.8 us (19%)
  local copies, waits for them, and re-layouts  15.9 us (8%)
  between operations  14.7 us (7%)
  matrix products  8.68 us (4%)
  other arithmetic  7.58 us (4%)
    psum x1, blocking collectives, per_device(): lax.psum((block_part, encoder_part), ('lon', 'lat'))  74.7 us
    unnamed x4, waiting for transfers between devices  17.9 us
    ppermute x5, starting transfers between devices, padded(): lax.ppermute(lax.slice_in_dim(block, 0, width, axis=dim), axis, backward)  12.4 us
    ppermute x6, starting transfers between devices, from_behind(): return lax.ppermute(block, axis, route)  11.3 us
    ppermute x5, starting transfers between devices, padded(): lax.ppermute(lax.slice_in_dim(block, block.shape[dim] - width, None, axis...  11 us
    ppermute x4, starting transfers between devices, passed_along(): return lax.ppermute(value, axis, pairs)  7.87 us
    unnamed x28, local copies, waits for them, and re-layouts  7.76 us
    ppermute x6, waiting for transfers between devices, from_behind(): return lax.ppermute(block, axis, route)  7.23 us
  transfers between devices with their start and end apart: 22, of which 12 were waited for; matrix products, arithmetic and copies ran while one was open for 5% of the time, Pallas kernels for 0%

commit v1 on v0

--- a/solution.py
+++ b/solution.py
@@ -196,7 +196,7 @@
             encoder_term.astype(jnp.bfloat16), "ch", scatter_dimension=1, tiled=True
         ).astype(jnp.float32),
     )
-    block_sum, encoder_sum = lax.psum((block_part, encoder_part), ("lon", "lat"))
+    block_sum, encoder_sum = lax.psum(lax.psum((block_part, encoder_part), "lat"), "lon")
     cells_total = cell_count * lax.axis_size("lon") * lax.axis_size(("lat", "ch"))
     normalizer = 1.0 / math.sqrt(cells_total)
     block_grads = (block_sum * normalizer).reshape(layers, basis_count * channels, own_width)

time: 205 us -> 228 us (1.11)
  waiting for transfers between devices: 39.8 us -> 101 us
  blocking collectives: 74.7 us -> 36.6 us
    psum x0 -> x1, waiting for transfers between devices: none -> 59.6 us  [per_device(): lax.psum(lax.psum((block_part, encoder_part), 'lat'), 'lon')]
    psum x1, blocking collectives: 74.7 us -> 36.6 us  [per_device(): lax.psum((block_part, encoder_part), 'lat')]
    unnamed x4 -> x5, waiting for transfers between devices: 17.9 us -> 19.5 us
    unnamed x28 -> x30, local copies, waits for them, and re-layouts: 7.76 us -> 6.85 us
  transfers between devices with their start and end apart: 22 -> 23, of which waited for: 12 -> 13; matrix products, arithmetic and copies ran while one was open for 5% -> 4% of each run, Pallas kernels for 0% -> 0%
where the time goes in v1:
time: 228 us; the launch traced here: 227 us
  waiting for transfers between devices  101 us (44%)
  starting transfers between devices  42.6 us (19%)
  blocking collectives  36.6 us (16%)
  local copies, waits for them, and re-layouts  15 us (7%)
  between operations  14.4 us (6%)
  other arithmetic  8.84 us (4%)
  matrix products  8.66 us (4%)
    psum x1, waiting for transfers between devices, per_device(): lax.psum(lax.psum((block_part, encoder_part), 'lat'), 'lon')  59.6 us
    psum x1, blocking collectives, per_device(): lax.psum((block_part, encoder_part), 'lat')  36.6 us
    unnamed x5, waiting for transfers between devices  19.5 us
    ppermute x5, starting transfers between devices, padded(): lax.ppermute(lax.slice_in_dim(block, 0, width, axis=dim), axis, backward)  12.4 us
    ppermute x6, starting transfers between devices, from_behind(): return lax.ppermute(block, axis, route)  11.3 us
    ppermute x5, starting transfers between devices, padded(): lax.ppermute(lax.slice_in_dim(block, block.shape[dim] - width, None, axis...  11 us
    ppermute x4, starting transfers between devices, passed_along(): return lax.ppermute(value, axis, pairs)  7.87 us
    ppermute x6, waiting for transfers between devices, from_behind(): return lax.ppermute(block, axis, route)  7.23 us
  transfers between devices with their start and end apart: 23, of which 13 were waited for; matrix products, arithmetic and copies ran while one was open for 4% of the time, Pallas kernels for 0%

profile of v1, /device:TPU:0, one launch (start us, length us, event | category | flops | bytes accessed | tf_op | source)
XLA Modules:
  0.0 227.1 jit_solution(14162801885096451170)
XLA Ops:
  7.2 1.0 fusion.64
  8.2 3.1 %collective-permute-start = (bf16[32,2,128]{2,1,0:T(2,128)(2,1)S(1)}, bf16[32,2,128]{2,1,0:T(2,128)(2,1)S(1)}, u32[]{:S(2)}, u32[]{:S(2)}) collective-permute-start(bf16[32,2,128]{2,1,0:T(2,128)(2,1)S(1)} %get-tuple-element.27), channel_id=1, source_target_pairs={{0,4},{4,8},{8,12},{12,0},{1,5},{5,9},{9,13},{13,1},{2,6},{6,10},{... | collective-permute-start | bytes 49160 | tf_op jit(solution)/shard_map/ppermute | solution.py:30
  11.3 2.1 collective-permute-start.1
  14.1 0.7 broadcast_compare_fusion
  14.8 0.8 select_bitcast_fusion
  16.3 1.8 slice.167
  20.8 1.0 add_convert_fusion
  22.5 1.5 collective-permute-start.2
  24.0 1.3 collective-permute-start.3
  25.3 3.5 %collective-permute-done.3 = bf16[1,8192]{1,0:T(2,128)(2,1)S(1)} collective-permute-done((bf16[1,8192]{1,0:T(2,128)(2,1)S(1)}, bf16[1,8192]{1,0:T(2,128)(2,1)S(1)}, u32[]{:S(2)}, u32[]{:S(2)}) %collective-permute-start.3) | collective-permute-done | bytes 16416 | tf_op jit(solution)/shard_map/ppermute | solution.py:20
  29.3 4.5 %collective-permute-start.4 = (bf16[1,16,256]{2,1,0:T(8,128)(2,1)S(1)}, bf16[1,16,256]{2,1,0:T(8,128)(2,1)S(1)}, u32[]{:S(2)}, u32[]{:S(2)}) collective-permute-start(bf16[1,16,256]{2,1,0:T(8,128)(2,1)S(1)} %get-tuple-element.35), channel_id=1, source_target_pairs={{0,1},{1,2},{2,3},{4,5},{5,6},{6,7},{8,9},{9,10},{10,11},{12,13},{... | collective-permute-start | bytes 24584 | tf_op jit(solution)/shard_map/ppermute | solution.py:30
  33.9 1.3 collective-permute-start.5
  35.6 1.4 collective-permute-done.5
  37.1 3.8 %collective-permute-start.7 = (bf16[18,8,256]{2,1,0:T(8,128)(2,1)S(1)}, bf16[18,8,256]{2,1,0:T(8,128)(2,1)S(1)}, u32[]{:S(2)}, u32[]{:S(2)}) collective-permute-start(bf16[18,8,256]{2,1,0:T(8,128)(2,1)S(1)} %get-tuple-element.32), channel_id=1, source_target_pairs={{4,0},{8,4},{12,8},{0,12},{5,1},{9,5},{13,9},{1,13},{6,2},{10,6},{... | collective-permute-start | bytes 221192 | tf_op jit(solution)/shard_map/ppermute | solution.py:33
  41.0 2.3 %collective-permute-done.6 = bf16[18,8,256]{2,1,0:T(8,128)(2,1)S(1)} collective-permute-done((bf16[18,8,256]{2,1,0:T(8,128)(2,1)S(1)}, bf16[18,8,256]{2,1,0:T(8,128)(2,1)S(1)}, u32[]{:S(2)}, u32[]{:S(2)}) %collective-permute-start.6) | collective-permute-done | bytes 73760 | tf_op jit(solution)/shard_map/ppermute | solution.py:30
  44.6 0.8 copy-done.1
  45.4 1.0 fusion.37
  46.5 3.2 %collective-permute-start.8 = (bf16[1,16,256]{2,1,0:T(8,128)(2,1)S(1)}, bf16[1,16,256]{2,1,0:T(8,128)(2,1)S(1)}, u32[]{:S(2)}, u32[]{:S(2)}) collective-permute-start(bf16[1,16,256]{2,1,0:T(8,128)(2,1)S(1)} %get-tuple-element.33), channel_id=1, source_target_pairs={{0,1},{1,2},{2,3},{4,5},{5,6},{6,7},{8,9},{9,10},{10,11},{12,13},{... | collective-permute-start | bytes 24584 | tf_op jit(solution)/shard_map/ppermute | solution.py:30
  49.7 1.3 collective-permute-start.9
  51.0 1.8 collective-permute-done.9
  52.9 3.9 %collective-permute-start.11 = (bf16[18,8,256]{2,1,0:T(8,128)(2,1)S(1)}, bf16[18,8,256]{2,1,0:T(8,128)(2,1)S(1)}, u32[]{:S(2)}, u32[]{:S(2)}) collective-permute-start(bf16[18,8,256]{2,1,0:T(8,128)(2,1)S(1)} %get-tuple-element.30), channel_id=1, source_target_pairs={{4,0},{8,4},{12,8},{0,12},{5,1},{9,5},{13,9},{1,13},{6,2},{10,6},{... | collective-permute-start | bytes 221192 | tf_op jit(solution)/shard_map/ppermute | solution.py:33
  56.8 2.4 %collective-permute-done.10 = bf16[18,8,256]{2,1,0:T(8,128)(2,1)S(1)} collective-permute-done((bf16[18,8,256]{2,1,0:T(8,128)(2,1)S(1)}, bf16[18,8,256]{2,1,0:T(8,128)(2,1)S(1)}, u32[]{:S(2)}, u32[]{:S(2)}) %collective-permute-start.10) | collective-permute-done | bytes 73760 | tf_op jit(solution)/shard_map/ppermute | solution.py:30
  61.0 1.1 fusion.35
  64.5 1.3 collective-permute-start.12
  65.8 2.7 %collective-permute-start.13 = (bf16[18,8,256]{2,1,0:T(8,128)(2,1)S(1)}, bf16[18,8,256]{2,1,0:T(8,128)(2,1)S(1)}, u32[]{:S(2)}, u32[]{:S(2)}) collective-permute-start(bf16[18,8,256]{2,1,0:T(8,128)(2,1)S(1)} %get-tuple-element.24), channel_id=1, source_target_pairs={{0,12},{4,0},{8,4},{12,8},{1,13},{5,1},{9,5},{13,9},{2,14},{6,2},{... | collective-permute-start | bytes 221192 | tf_op jit(solution)/shard_map/ppermute | solution.py:14
  68.5 2.4 %collective-permute-done.12 = bf16[18,8,256]{2,1,0:T(8,128)(2,1)S(1)} collective-permute-done((bf16[18,8,256]{2,1,0:T(8,128)(2,1)S(1)}, bf16[18,8,256]{2,1,0:T(8,128)(2,1)S(1)}, u32[]{:S(2)}, u32[]{:S(2)}) %collective-permute-start.12) | collective-permute-done | bytes 73760 | tf_op jit(solution)/shard_map/ppermute | solution.py:14
  70.8 1.9 collective-permute-done.13
  72.8 2.1 collective-permute-start.14
  74.9 1.3 collective-permute-start.15
  76.2 1.8 collective-permute-done.15
  78.2 1.1 convolution_convert_fusion.3
  79.3 1.4 reshape.128
  81.8 1.1 collective-permute-start.16
  82.9 2.8 %collective-permute-start.17 = (bf16[18,8,256]{2,1,0:T(8,128)(2,1)S(1)}, bf16[18,8,256]{2,1,0:T(8,128)(2,1)S(1)}, u32[]{:S(2)}, u32[]{:S(2)}) collective-permute-start(bf16[18,8,256]{2,1,0:T(8,128)(2,1)S(1)} %get-tuple-element.20), channel_id=1, source_target_pairs={{0,12},{4,0},{8,4},{12,8},{1,13},{5,1},{9,5},{13,9},{2,14},{6,2},{... | collective-permute-start | bytes 221192 | tf_op jit(solution)/shard_map/ppermute | solution.py:14
  85.7 2.4 %collective-permute-done.16 = bf16[18,8,256]{2,1,0:T(8,128)(2,1)S(1)} collective-permute-done((bf16[18,8,256]{2,1,0:T(8,128)(2,1)S(1)}, bf16[18,8,256]{2,1,0:T(8,128)(2,1)S(1)}, u32[]{:S(2)}, u32[]{:S(2)}) %collective-permute-start.16) | collective-permute-done | bytes 73760 | tf_op jit(solution)/shard_map/ppermute | solution.py:14
  88.2 3.7 %collective-permute-start.18 = (f32[1,16,256]{2,1,0:T(8,128)S(1)}, f32[1,16,256]{2,1,0:T(8,128)S(1)}, u32[]{:S(2)}, u32[]{:S(2)}) collective-permute-start(f32[1,16,256]{2,1,0:T(8,128)S(1)} %get-tuple-element.17), channel_id=1, source_target_pairs={{0,1},{1,2},{2,3},{4,5},{5,6},{6,7},{8,9},{9,10},{10,11},{12,13},{... | collective-permute-start | bytes 49160 | tf_op jit(solution)/shard_map/ppermute | solution.py:20
  91.9 1.4 collective-permute-start.19
  93.4 1.9 collective-permute-done.19
  95.6 0.8 copy.106
  97.3 1.4 copy.104
  98.8 8.1 %reduce-scatter.9.cloned.1.call-done = bf16[128,512]{1,0:T(8,128)(2,1)} async-done(((bf16[256,512]{1,0:T(8,128)(2,1)}), bf16[128,512]{1,0:T(8,128)(2,1)}) %reduce-scatter.9.cloned.1.call-update) | async-done | bytes 131088
  107.0 1.0 copy.107
  108.0 11.3 %reduce-scatter.7.cloned.1.call-done = bf16[128,2048]{1,0:T(8,128)(2,1)} async-done(((bf16[256,2048]{1,0:T(8,128)(2,1)}), bf16[128,2048]{1,0:T(8,128)(2,1)}) %reduce-scatter.7.cloned.1.call-update) | async-done | bytes 524304
  119.3 1.3 copy.105
  120.6 36.6 %all-reduce.22 = (f32[2048,128]{1,0:T(8,128)}, f32[512,128]{1,0:T(8,128)}) all-reduce(bf16[2048,128]{1,0:T(8,128)(2,1)S(1)} %copy.105, bf16[512,128]{1,0:T(8,128)(2,1)S(1)} %copy.107), channel_id=1, replica_groups=mesh['ens'=2,'lon'=4,'lat'=2,'ch'=2] {'lat'}, use_global_device_ids=true, to_apply=%region_1.2 | all-reduce | flops 327680 | bytes 1966080 | tf_op jit(solution)/shard_map/psum | solution.py:199
  158.0 59.6 %all-reduce.21.cloned.1.call-done = (f32[2048,128]{1,0:T(8,128)}, f32[512,128]{1,0:T(8,128)}) async-done(((f32[2048,128]{1,0:T(8,128)}, f32[512,128]{1,0:T(8,128)}), (f32[2048,128]{1,0:T(8,128)}, f32[512,128]{1,0:T(8,128)})) %all-reduce.21.cloned.1.call-update) | async-done | bytes 1310736 | tf_op jit(solution)/shard_map/psum | solution.py:199
  217.5 2.3 %broadcast_multiply_fusion = f32[2048,128]{1,0:T(8,128)} fusion(f32[2048,128]{1,0:T(8,128)} %get-tuple-element.4), kind=kLoop, calls=%fused_computation.34 | loop fusion | flops 262144 | bytes 2097152 | tf_op jit(solution)/shard_map/mul | solution.py:202
  219.9 0.7 broadcast_multiply_fusion.1
  (112 shorter events, 14.4 us)
Async XLA Ops:
  7.2 21.9 %copy-start = (bf16[512,256]{1,0:T(8,128)(2,1)S(1)}, bf16[512,256]{1,0:T(8,128)(2,1)}, u32[]{:S(2)}) copy-start(bf16[512,256]{1,0:T(8,128)(2,1)} %param.11) | copy-start | bytes 786436
  7.2 11.5 %copy-start.3 = (bf16[32,32,128]{2,1,0:T(8,128)(2,1)S(1)}, bf16[32,32,128]{2,1,0:T(8,128)(2,1)}, u32[]{:S(2)}) copy-start(bf16[32,32,128]{2,1,0:T(8,128)(2,1)} %param.8) | copy-start | bytes 786436
  7.2 99.8 %reduce-scatter.9.cloned.1.call-start = ((), (), s32[]{:S(2)}) async-start(), calls=%async_computation.3 | async-start | bytes 393216
  8.2 10.4 %collective-permute-start = (bf16[32,2,128]{2,1,0:T(2,128)(2,1)S(1)}, bf16[32,2,128]{2,1,0:T(2,128)(2,1)S(1)}, u32[]{:S(2)}, u32[]{:S(2)}) collective-permute-start(bf16[32,2,128]{2,1,0:T(2,128)(2,1)S(1)} %get-tuple-element.27), channel_id=1, source_target_pairs={{0,4},{4,8},{8,12},{12,0},{1,5},{5,9},{9,13},{13,1},{2,6},{6,10},{... | collective-permute-start | bytes 49160 | tf_op jit(solution)/shard_map/ppermute | solution.py:30
  11.3 7.3 %collective-permute-start.1 = (bf16[32,2,128]{2,1,0:T(2,128)(2,1)S(1)}, bf16[32,2,128]{2,1,0:T(2,128)(2,1)S(1)}, u32[]{:S(2)}, u32[]{:S(2)}) collective-permute-start(bf16[32,2,128]{2,1,0:T(2,128)(2,1)S(1)} %get-tuple-element.28), channel_id=1, source_target_pairs={{4,0},{8,4},{12,8},{0,12},{5,1},{9,5},{13,9},{1,13},{6,2},{10,6},{... | collective-permute-start | bytes 49160 | tf_op jit(solution)/shard_map/ppermute | solution.py:33
  22.5 2.8 %collective-permute-start.2 = (bf16[1,8192]{1,0:T(2,128)(2,1)S(1)}, bf16[1,8192]{1,0:T(2,128)(2,1)S(1)}, u32[]{:S(2)}, u32[]{:S(2)}) collective-permute-start(bf16[1,8192]{1,0:T(2,128)(2,1)S(1)} %get-tuple-element.15), channel_id=1, source_target_pairs={{0,1},{1,2},{2,3},{4,5},{5,6},{6,7},{8,9},{9,10},{10,11},{12,13},{... | collective-permute-start | bytes 49160 | tf_op jit(solution)/shard_map/ppermute | solution.py:20
  24.0 4.8 %collective-permute-start.3 = (bf16[1,8192]{1,0:T(2,128)(2,1)S(1)}, bf16[1,8192]{1,0:T(2,128)(2,1)S(1)}, u32[]{:S(2)}, u32[]{:S(2)}) collective-permute-start(bf16[1,8192]{1,0:T(2,128)(2,1)S(1)} %get-tuple-element.16), channel_id=1, source_target_pairs={{1,0},{2,1},{3,2},{5,4},{6,5},{7,6},{9,8},{10,9},{11,10},{13,12},{... | collective-permute-start | bytes 49160 | tf_op jit(solution)/shard_map/ppermute | solution.py:20
  29.3 6.2 %collective-permute-start.4 = (bf16[1,16,256]{2,1,0:T(8,128)(2,1)S(1)}, bf16[1,16,256]{2,1,0:T(8,128)(2,1)S(1)}, u32[]{:S(2)}, u32[]{:S(2)}) collective-permute-start(bf16[1,16,256]{2,1,0:T(8,128)(2,1)S(1)} %get-tuple-element.35), channel_id=1, source_target_pairs={{0,1},{1,2},{2,3},{4,5},{5,6},{6,7},{8,9},{9,10},{10,11},{12,13},{... | collective-permute-start | bytes 24584 | tf_op jit(solution)/shard_map/ppermute | solution.py:30
  33.9 3.1 %collective-permute-start.5 = (bf16[1,16,256]{2,1,0:T(8,128)(2,1)S(1)}, bf16[1,16,256]{2,1,0:T(8,128)(2,1)S(1)}, u32[]{:S(2)}, u32[]{:S(2)}) collective-permute-start(bf16[1,16,256]{2,1,0:T(8,128)(2,1)S(1)} %get-tuple-element.36), channel_id=1, source_target_pairs={{1,0},{2,1},{3,2},{5,4},{6,5},{7,6},{9,8},{10,9},{11,10},{13,12},{... | collective-permute-start | bytes 24584 | tf_op jit(solution)/shard_map/ppermute | solution.py:33
  37.0 6.3 %collective-permute-start.6 = (bf16[18,8,256]{2,1,0:T(8,128)(2,1)S(1)}, bf16[18,8,256]{2,1,0:T(8,128)(2,1)S(1)}, u32[]{:S(2)}, u32[]{:S(2)}) collective-permute-start(bf16[18,8,256]{2,1,0:T(8,128)(2,1)S(1)} %get-tuple-element.31), channel_id=1, source_target_pairs={{0,4},{4,8},{8,12},{12,0},{1,5},{5,9},{9,13},{13,1},{2,6},{6,10},{... | collective-permute-start | bytes 221192 | tf_op jit(solution)/shard_map/ppermute | solution.py:30
  37.1 6.2 %collective-permute-start.7 = (bf16[18,8,256]{2,1,0:T(8,128)(2,1)S(1)}, bf16[18,8,256]{2,1,0:T(8,128)(2,1)S(1)}, u32[]{:S(2)}, u32[]{:S(2)}) collective-permute-start(bf16[18,8,256]{2,1,0:T(8,128)(2,1)S(1)} %get-tuple-element.32), channel_id=1, source_target_pairs={{4,0},{8,4},{12,8},{0,12},{5,1},{9,5},{13,9},{1,13},{6,2},{10,6},{... | collective-permute-start | bytes 221192 | tf_op jit(solution)/shard_map/ppermute | solution.py:33
  44.2 1.2 copy-start.1
  46.5 4.5 %collective-permute-start.8 = (bf16[1,16,256]{2,1,0:T(8,128)(2,1)S(1)}, bf16[1,16,256]{2,1,0:T(8,128)(2,1)S(1)}, u32[]{:S(2)}, u32[]{:S(2)}) collective-permute-start(bf16[1,16,256]{2,1,0:T(8,128)(2,1)S(1)} %get-tuple-element.33), channel_id=1, source_target_pairs={{0,1},{1,2},{2,3},{4,5},{5,6},{6,7},{8,9},{9,10},{10,11},{12,13},{... | collective-permute-start | bytes 24584 | tf_op jit(solution)/shard_map/ppermute | solution.py:30
  49.7 3.1 %collective-permute-start.9 = (bf16[1,16,256]{2,1,0:T(8,128)(2,1)S(1)}, bf16[1,16,256]{2,1,0:T(8,128)(2,1)S(1)}, u32[]{:S(2)}, u32[]{:S(2)}) collective-permute-start(bf16[1,16,256]{2,1,0:T(8,128)(2,1)S(1)} %get-tuple-element.34), channel_id=1, source_target_pairs={{1,0},{2,1},{3,2},{5,4},{6,5},{7,6},{9,8},{10,9},{11,10},{13,12},{... | collective-permute-start | bytes 24584 | tf_op jit(solution)/shard_map/ppermute | solution.py:33
  52.9 6.3 %collective-permute-start.10 = (bf16[18,8,256]{2,1,0:T(8,128)(2,1)S(1)}, bf16[18,8,256]{2,1,0:T(8,128)(2,1)S(1)}, u32[]{:S(2)}, u32[]{:S(2)}) collective-permute-start(bf16[18,8,256]{2,1,0:T(8,128)(2,1)S(1)} %get-tuple-element.29), channel_id=1, source_target_pairs={{0,4},{4,8},{8,12},{12,0},{1,5},{5,9},{9,13},{13,1},{2,6},{6,10},{... | collective-permute-start | bytes 221192 | tf_op jit(solution)/shard_map/ppermute | solution.py:30
  52.9 6.2 %collective-permute-start.11 = (bf16[18,8,256]{2,1,0:T(8,128)(2,1)S(1)}, bf16[18,8,256]{2,1,0:T(8,128)(2,1)S(1)}, u32[]{:S(2)}, u32[]{:S(2)}) collective-permute-start(bf16[18,8,256]{2,1,0:T(8,128)(2,1)S(1)} %get-tuple-element.30), channel_id=1, source_target_pairs={{4,0},{8,4},{12,8},{0,12},{5,1},{9,5},{13,9},{1,13},{6,2},{10,6},{... | collective-permute-start | bytes 221192 | tf_op jit(solution)/shard_map/ppermute | solution.py:33
  60.1 0.9 copy-start.10
  62.0 0.7 copy-start.4
  64.4 13.6 %copy-start.11 = (bf16[16,16,256]{2,1,0:T(8,128)(2,1)S(1)}, bf16[16,16,256]{2,1,0:T(8,128)(2,1)}, u32[]{:S(2)}) copy-start(bf16[16,16,256]{2,1,0:T(8,128)(2,1)} %param.15) | copy-start | bytes 393220
  64.4 13.6 %copy-start.8 = (f32[256,256]{1,0:T(8,128)S(1)}, f32[256,256]{1,0:T(8,128)}, u32[]{:S(2)}) copy-start(f32[256,256]{1,0:T(8,128)} %get-tuple-element.45) | copy-start | bytes 786436
  64.5 6.4 %collective-permute-start.12 = (bf16[18,8,256]{2,1,0:T(8,128)(2,1)S(1)}, bf16[18,8,256]{2,1,0:T(8,128)(2,1)S(1)}, u32[]{:S(2)}, u32[]{:S(2)}) collective-permute-start(bf16[18,8,256]{2,1,0:T(8,128)(2,1)S(1)} %get-tuple-element.23), channel_id=1, source_target_pairs={{0,4},{4,8},{8,12},{12,0},{1,5},{5,9},{9,13},{13,1},{2,6},{6,10},{... | collective-permute-start | bytes 221192 | tf_op jit(solution)/shard_map/ppermute | solution.py:14
  65.8 7.0 %collective-permute-start.13 = (bf16[18,8,256]{2,1,0:T(8,128)(2,1)S(1)}, bf16[18,8,256]{2,1,0:T(8,128)(2,1)S(1)}, u32[]{:S(2)}, u32[]{:S(2)}) collective-permute-start(bf16[18,8,256]{2,1,0:T(8,128)(2,1)S(1)} %get-tuple-element.24), channel_id=1, source_target_pairs={{0,12},{4,0},{8,4},{12,8},{1,13},{5,1},{9,5},{13,9},{2,14},{6,2},{... | collective-permute-start | bytes 221192 | tf_op jit(solution)/shard_map/ppermute | solution.py:14
  72.8 5.4 %copy-start.2 = (bf16[2,1024,256]{2,1,0:T(8,128)(2,1)S(1)}, bf16[2,1024,256]{2,1,0:T(8,128)(2,1)}, u32[]{:S(2)}) copy-start(bf16[2,1024,256]{2,1,0:T(8,128)(2,1)} %param.14) | copy-start | bytes 3145732
  72.8 3.4 %collective-permute-start.14 = (f32[1,16,256]{2,1,0:T(8,128)S(1)}, f32[1,16,256]{2,1,0:T(8,128)S(1)}, u32[]{:S(2)}, u32[]{:S(2)}) collective-permute-start(f32[1,16,256]{2,1,0:T(8,128)S(1)} %get-tuple-element.21), channel_id=1, source_target_pairs={{0,1},{1,2},{2,3},{4,5},{5,6},{6,7},{8,9},{9,10},{10,11},{12,13},{... | collective-permute-start | bytes 49160 | tf_op jit(solution)/shard_map/ppermute | solution.py:20
  74.9 3.1 %collective-permute-start.15 = (f32[1,16,256]{2,1,0:T(8,128)S(1)}, f32[1,16,256]{2,1,0:T(8,128)S(1)}, u32[]{:S(2)}, u32[]{:S(2)}) collective-permute-start(f32[1,16,256]{2,1,0:T(8,128)S(1)} %get-tuple-element.22), channel_id=1, source_target_pairs={{1,0},{2,1},{3,2},{5,4},{6,5},{7,6},{9,8},{10,9},{11,10},{13,12},{... | collective-permute-start | bytes 49160 | tf_op jit(solution)/shard_map/ppermute | solution.py:20
  81.8 6.3 %collective-permute-start.16 = (bf16[18,8,256]{2,1,0:T(8,128)(2,1)S(1)}, bf16[18,8,256]{2,1,0:T(8,128)(2,1)S(1)}, u32[]{:S(2)}, u32[]{:S(2)}) collective-permute-start(bf16[18,8,256]{2,1,0:T(8,128)(2,1)S(1)} %get-tuple-element.19), channel_id=1, source_target_pairs={{0,4},{4,8},{8,12},{12,0},{1,5},{5,9},{9,13},{13,1},{2,6},{6,10},{... | collective-permute-start | bytes 221192 | tf_op jit(solution)/shard_map/ppermute | solution.py:14
  82.9 5.2 %collective-permute-start.17 = (bf16[18,8,256]{2,1,0:T(8,128)(2,1)S(1)}, bf16[18,8,256]{2,1,0:T(8,128)(2,1)S(1)}, u32[]{:S(2)}, u32[]{:S(2)}) collective-permute-start(bf16[18,8,256]{2,1,0:T(8,128)(2,1)S(1)} %get-tuple-element.20), channel_id=1, source_target_pairs={{0,12},{4,0},{8,4},{12,8},{1,13},{5,1},{9,5},{13,9},{2,14},{6,2},{... | collective-permute-start | bytes 221192 | tf_op jit(solution)/shard_map/ppermute | solution.py:14
  88.2 5.2 %collective-permute-start.18 = (f32[1,16,256]{2,1,0:T(8,128)S(1)}, f32[1,16,256]{2,1,0:T(8,128)S(1)}, u32[]{:S(2)}, u32[]{:S(2)}) collective-permute-start(f32[1,16,256]{2,1,0:T(8,128)S(1)} %get-tuple-element.17), channel_id=1, source_target_pairs={{0,1},{1,2},{2,3},{4,5},{5,6},{6,7},{8,9},{9,10},{10,11},{12,13},{... | collective-permute-start | bytes 49160 | tf_op jit(solution)/shard_map/ppermute | solution.py:20
  91.9 4.6 %copy-start.5 = (bf16[256,256]{1,0:T(8,128)(2,1)S(1)}, bf16[256,256]{1,0:T(8,128)(2,1)}, u32[]{:S(2)}) copy-start(bf16[256,256]{1,0:T(8,128)(2,1)} %copy-done.4) | copy-start | bytes 393220
  91.9 3.3 %collective-permute-start.19 = (f32[1,16,256]{2,1,0:T(8,128)S(1)}, f32[1,16,256]{2,1,0:T(8,128)S(1)}, u32[]{:S(2)}, u32[]{:S(2)}) collective-permute-start(f32[1,16,256]{2,1,0:T(8,128)S(1)} %get-tuple-element.18), channel_id=1, source_target_pairs={{1,0},{2,1},{3,2},{5,4},{6,5},{7,6},{9,8},{10,9},{11,10},{13,12},{... | collective-permute-start | bytes 49160 | tf_op jit(solution)/shard_map/ppermute | solution.py:20
  95.3 1.6 copy-start.6
  96.5 22.8 %reduce-scatter.7.cloned.1.call-start = ((), (), s32[]{:S(2)}) async-start(), calls=%async_computation.2 | async-start | bytes 1572864
  98.8 118.8 %all-reduce.21.cloned.1.call-start = ((), (), s32[]{:S(2)}) async-start(), calls=%async_computation.4 | async-start | bytes 2621440 | tf_op jit(solution)/shard_map/psum | solution.py:199
  120.6 36.7 %copy-start.7 = (f32[256,256]{1,0:T(8,128)S(1)}, f32[256,256]{1,0:T(8,128)}, u32[]{:S(2)}) copy-start(f32[256,256]{1,0:T(8,128)} %get-tuple-element.26) | copy-start | bytes 786436
  217.5 2.3 %copy-start.9 = (f32[512,128]{1,0:T(8,128)S(1)}, f32[512,128]{1,0:T(8,128)}, u32[]{:S(2)}) copy-start(f32[512,128]{1,0:T(8,128)} %get-tuple-element.5) | copy-start | bytes 786436
Sparse Core Ops, SparseCore 0:
  96.6 10.3 reduce-scatter.8
  109.8 9.4 reduce-scatter.6
  157.4 60.0 all-reduce.20
